TPU v7x, 32 devices: a whole 2x2x4 slice. The times are simulated.
32 devices in a mesh: group: 2 (over y), frame: 8 (over z, x), row: 2 (over core).
Axes of the slice: x: 2, y: 2, z: 4, core: 2. Of those that a mesh axis runs over, the one named last changes fastest.
Arguments:
- latents: bfloat16 [16, 8, 32, 1120], P(('group', 'frame'), 'row'), parts along dimension 0, may hold values from -24 to 24
- spatial_weights: bfloat16 [4, 10, 112, 112], replicated, may hold values from -0.5 to 0.5
- causal_weights: bfloat16 [4, 10, 112, 112], replicated, may hold values from -0.5 to 0.5
Outputs:
- updated_latents: bfloat16 [16, 8, 32, 1120], P(('group', 'frame'), None, None, 'row'), parts along dimension 0
There are 2 independent parts, one for each index of `group`. A program takes and returns all parts, laid end to end along the dimension named above; an argument that names none is the same for every part. Nothing has to cross between parts.
All inputs are finite; a program needn't handle non-finite values.
Results may differ from a plain program's by a relative error of at most 0.0047.
The roundings to bfloat16 on the way count: a program that leaves them out, or rounds other values in their place, can miss the bound.
Values may be sent and summed in bfloat16 or wider, within the bound.
No kernel may reach another device: no remote copies, remote signals or barrier semaphores. Data moves between devices by JAX's collectives and lax.ppermute only.
A program may use at most 64 MiB of HBM per device.

v0:
```python
import jax
import jax.numpy as jnp
from jax import lax
from jax.sharding import PartitionSpec as P


def prefix(x, axis, join, neutral):
    place = lax.axis_index(axis)
    gathered = lax.all_gather(x.astype(jnp.bfloat16), axis)
    state = jnp.zeros_like(x) + jnp.asarray(neutral, x.dtype)

    def one(turn, state):
        return join(state, lax.dynamic_index_in_dim(gathered, turn, 0, False).astype(x.dtype))

    return lax.fori_loop(0, place, one, state)


def normalize(frame_block):
    feat_width = frame_block.shape[-1]
    flat_rows = frame_block.reshape(-1, feat_width).astype(jnp.float32)
    normed = flat_rows * lax.rsqrt(jnp.mean(flat_rows * flat_rows, axis=-1, keepdims=True) + 1e-06)
    return normed.astype(jnp.bfloat16).reshape(frame_block.shape)


def project(normed, weights):
    head_count = weights.shape[1]
    head_size = weights.shape[2]
    normed = normed.reshape(-1, head_count, head_size)
    mapped = jnp.einsum("thd,khde->kthe", normed, weights, preferred_element_type=jnp.float32)
    queries = jax.nn.relu(mapped[0]).astype(jnp.bfloat16)
    key_rows = jax.nn.relu(mapped[1]).astype(jnp.bfloat16)
    value_rows = mapped[2].astype(jnp.bfloat16)
    gating = jax.nn.sigmoid(mapped[3])
    return (queries, key_rows, value_rows, gating)


def local_state(key_rows, value_rows):
    return jnp.einsum("thd,the->hde", key_rows, value_rows, preferred_element_type=jnp.float32)


def attend(queries, state):
    return jnp.einsum(
        "thd,hde->the", queries.astype(jnp.float32), state, precision=lax.Precision.HIGHEST
    )


def finish(frame_block, gating, attended):
    inv_rms = lax.rsqrt(jnp.mean(attended * attended, axis=-1, keepdims=True) + 1e-05)
    branch = (gating * attended * inv_rms).reshape(frame_block.shape)
    return (frame_block.astype(jnp.float32) + branch).astype(jnp.bfloat16)


def add_states(earlier, later):
    return earlier + later


def body(latents, spatial_weights, causal_weights):
    queries, key_rows, value_rows, gating = project(normalize(latents), spatial_weights)
    frame_state = lax.psum(local_state(key_rows, value_rows), "row")
    mixed_video = finish(latents, gating, attend(queries, frame_state))
    normed_c = normalize(mixed_video)
    mixed_heads, normed_heads = (
        lax.all_to_all(mixed_video, "row", split_axis=3, concat_axis=1, tiled=True),
        lax.all_to_all(normed_c, "row", split_axis=3, concat_axis=1, tiled=True),
    )
    head_part = causal_weights.shape[1] // lax.axis_size("row")
    head_start = lax.axis_index("row") * head_part
    local_weights = lax.dynamic_slice_in_dim(causal_weights, head_start, head_part, 1)
    queries, key_rows, value_rows, gating = project(normed_heads, local_weights)
    own_state = local_state(key_rows, value_rows)
    flat_state = own_state.reshape(-1, 128)
    earlier_flat = prefix(flat_state, "frame", add_states, jnp.zeros_like(flat_state))
    earlier = earlier_flat.reshape(own_state.shape)
    attended = attend(queries, earlier + own_state)
    return finish(mixed_heads, gating, attended)


def solution(mesh):
    in_specs = (P(("group", "frame"), "row", None, None), P(), P())
    out_specs = P(("group", "frame"), None, None, "row")
    return jax.shard_map(body, mesh=mesh, in_specs=in_specs, out_specs=out_specs, check_vma=False)
```

profile of v0, /device:TPU:27, one launch (start us, length us, event | category | flops | bytes accessed | tf_op | source)
XLA Modules:
  0.0 119.3 jit_solution(12640229504760504047)
XLA Ops:
  6.5 0.0 copy-start
  6.5 0.0 all-reduce.2.cloned.1.call-start
  6.5 1.6 %reshape.152 = f32[128,10,112]{2,1,0:T(8,128)S(1)} reshape(bf16[1,4,32,1120]{3,2,1,0:T(8,128)(2,1)} %param.5) | data formatting | bytes 860160 | tf_op jit(solution)/shard_map/convert_element_type | solution.py:20
  8.2 1.1 multiply_reduce_fusion
  9.3 0.1 rsqrt.36
  9.4 0.2 fusion.20
  9.6 0.0 copy-done
  9.6 0.5 convolution_bitcast_fusion.1
  10.1 1.1 fusion.24
  11.3 0.0 all-reduce.2.cloned.1.call-update
  11.3 20.5 %all-reduce.2.cloned.1.call-done = f32[10,112,112]{2,1,0:T(8,128)} async-done(((f32[10,112,112]{2,1,0:T(8,128)}), f32[10,112,112]{2,1,0:T(8,128)}) %all-reduce.2.cloned.1.call-update) | async-done | bytes 501776 | tf_op jit(solution)/shard_map/psum | solution.py:59
  31.8 1.7 %multiply_reduce_fusion.2 = (f32[128,10]{0,1:T(8,128)S(1)}, f32[128,10,112]{0,2,1:T(8,128)S(1)}) fusion(f32[10,112,112]{2,1,0:T(8,128)} %all-reduce.2.cloned.1.call-done, f32[4,128,10,112]{1,3,0,2:T(8,128)S(1)} %convolution_bitcast_fusion.1), kind=kOutput, calls=%fused_computation.40 | convolution fusion | flops 193391360 | bytes 1367040 | tf_op jit(solution)/shard_map/thd,hde->the/dot_general | solution.py:42
  33.5 1.0 fusion.18
  34.5 0.0 copy-start.2
  34.5 1.6 %copy.24 = f32[128,10,112]{2,1,0:T(8,128)S(1)} copy(f32[128,10,112]{0,2,1:T(8,128)} %fusion.18) | data formatting | bytes 1146880 | tf_op jit(solution)/shard_map/mul | solution.py:49
  36.1 0.3 reshape.147
  36.4 0.0 copy-done.2
  36.4 0.2 fusion.1
  36.6 1.4 %copy.25 = bf16[1,4,32,1120]{2,1,0,3:T(4,128)(2,1)S(1)} copy(bf16[1,4,32,1120]{3,2,1,0:T(8,128)(2,1)S(1)} %get-tuple-element.38) | data formatting | bytes 573440 | tf_op jit(solution)/shard_map/convert_element_type | solution.py:50
  38.0 0.8 fusion.2
  38.8 2.2 %copy.28 = bf16[1,4,32,1120]{2,1,0,3:T(4,128)(2,1)S(1)} copy(bf16[1,4,32,1120]{3,2,1,0:T(8,128)(2,1)} %fusion.2) | data formatting | bytes 573440 | tf_op jit(solution)/shard_map/convert_element_type | solution.py:22
  41.0 1.8 %reshape.159 = bf16[2,2,35840]{2,1,0:T(2,128)(2,1)} reshape(bf16[1120,1,4,32]{3,2,1,0:T(4,128)(2,1)S(1)} %bitcast.72) | data formatting | bytes 573440
  42.8 5.7 %all_to_all.24 = bf16[2,2,35840]{2,1,0:T(2,128)(2,1)} all-to-all(bf16[2,2,35840]{2,1,0:T(2,128)(2,1)} %reshape.159), channel_id=1, replica_groups=mesh['group'=2,'frame'=8,'row'=2] {'row'}, dimensions={0} | all-to-all | bytes 573440 | tf_op jit(solution)/shard_map/all_to_all | solution.py:64
  48.5 1.7 %reshape.160 = bf16[1120,1,4,32]{3,2,1,0:T(4,128)(2,1)S(1)} reshape(bf16[2,2,35840]{2,1,0:T(2,128)(2,1)} %all_to_all.24) | data formatting | bytes 573440
  50.2 1.4 %copy.29 = bf16[1,4,32,2,560]{4,2,1,3,0:T(8,128)(2,1)} copy(bf16[1,4,32,2,560]{2,1,4,3,0:T(4,128)(2,1)S(1)} %bitcast.73) | data formatting | bytes 573440 | tf_op jit(solution)/shard_map/all_to_all | solution.py:64
  51.5 1.4 %reshape.148 = bf16[256,5,112]{2,1,0:T(8,128)(2,1)S(1)} reshape(bf16[1,2,4,32,560]{4,3,2,1,0:T(8,128)(2,1)} %bitcast.76) | data formatting | bytes 573440 | tf_op jit(solution)/shard_map/reshape | solution.py:28
  52.9 1.6 %convolution_bitcast_fusion = f32[4,256,5,112]{1,3,0,2:T(8,128)S(1)} fusion(bf16[256,5,112,1]{2,1,0,3:T(8,128)(2,1)S(1)} %bitcast.75, bf16[4,10,112,112]{3,2,1,0:T(8,128)(2,1)} %param.7, s32[]{:T(128)S(6)} %select_n.7), kind=kOutput, calls=%fused_computation.1 | convolution fusion | flops 128450560 | bytes 3153924 | tf_op jit(solution)/shard_map/thd,khde->kthe/dot_general | solution.py:29
  54.5 0.0 copy-start.1
  54.5 1.4 %copy-done.1 = f32[4,256,5,112]{1,3,0,2:T(8,128)} copy-done((f32[4,256,5,112]{1,3,0,2:T(8,128)}, f32[4,256,5,112]{1,3,0,2:T(8,128)S(1)}, u32[]{:S(2)}) %copy-start.1) | copy-done | bytes 2293784
  55.9 0.2 fusion.46
  56.1 0.3 convert_element_type.131
  56.4 28.5 %all_gather.4 = bf16[8,490,128]{2,1,0:T(8,128)(2,1)} all-gather(bf16[1,490,128]{2,1,0:T(8,128)(2,1)S(1)} %convert_element_type.131), channel_id=1, replica_groups=mesh['group'=2,'frame'=8,'row'=2] {'frame'}, dimensions={0}, use_global_device_ids=true | all-gather | bytes 1128960 | tf_op jit(solution)/shard_map/all_gather | solution.py:9
  84.9 6.8 %while.10 = (s32[]{:T(128)}, f32[490,128]{1,0:T(8,128)S(1)}, s32[]{:T(128)}, bf16[8,490,128]{2,1,0:T(8,128)(2,1)}, s32[]{:T(128)}, /*index=5*/s32[]{:T(128)}, s32[]{:T(128)}) while((s32[]{:T(128)}, f32[490,128]{1,0:T(8,128)S(1)}, s32[]{:T(128)}, bf16[8,490,128]{2,1,0:T(8,128)(2,1)}, s32[]{:T(128)}, /*index=5*/s32[]{:T(128)}, s32[]{:T(128)}) %tuple.22), condition=%wide.region_5.6_spmd, body=%wide.region_4.5_spmd.sunk | while | flops 125445 | bytes 627315 | solution.py:15
  85.0 0.9 convert_add_fusion.2
  85.9 0.9 convert_add_fusion.2
  86.9 0.9 convert_add_fusion.2
  87.9 0.9 convert_add_fusion.2
  88.8 0.9 convert_add_fusion.2
  89.8 0.9 convert_add_fusion.2
  90.8 0.9 convert_add_fusion.2
  91.7 0.2 reshape.149
  91.9 1.5 %multiply_reduce_fusion.1 = (f32[256,5]{0,1:T(8,128)S(1)}, f32[256,5,112]{0,2,1:T(8,128)S(1)}) fusion(f32[4,256,5,112]{1,3,0,2:T(8,128)} %copy-done.1, f32[5,112,112]{2,1,0:T(8,128)S(1)} %reshape.149, f32[5,112,112]{2,1,0:T(8,128)S(1)} %get-tuple-element.42), kind=kOutput, calls=%fused_computation.39 | convolution fusion | flops 193454080 | bytes 1367040 | tf_op jit(solution)/shard_map/thd,hde->the/dot_general | solution.py:42
  93.5 2.0 %fusion.10 = f32[256,5,112]{0,2,1:T(8,128)} fusion(f32[256,5,112]{0,2,1:T(8,128)S(1)} %get-tuple-element.44, f32[4,256,5,112]{1,3,0,2:T(8,128)} %copy-done.1, f32[256,5]{0,1:T(8,128)S(1)} %add_rsqrt_fusion), kind=kLoop, calls=%fused_computation.25 | loop fusion | flops 716800 | bytes 1725440 | tf_op jit(solution)/shard_map/mul | solution.py:49
  95.5 1.5 %copy.32 = f32[256,5,112]{2,1,0:T(8,128)S(1)} copy(f32[256,5,112]{0,2,1:T(8,128)} %fusion.10) | data formatting | bytes 1146880 | tf_op jit(solution)/shard_map/mul | solution.py:49
  97.0 1.1 reshape.150
  98.0 1.1 reshape.157
  99.2 10.2 %all_to_all.25 = bf16[2,2,35840]{2,1,0:T(2,128)(2,1)S(1)} all-to-all(bf16[2,2,35840]{2,1,0:T(2,128)(2,1)S(1)} %reshape.157), channel_id=1, replica_groups=mesh['group'=2,'frame'=8,'row'=2] {'row'}, dimensions={0} | all-to-all | bytes 573440 | tf_op jit(solution)/shard_map/all_to_all | solution.py:63
  109.3 0.6 reshape.158
  109.9 0.7 copy.26
  110.6 1.9 %add_convert_fusion = bf16[1,8,32,560]{3,2,1,0:T(8,128)(2,1)} fusion(f32[1,8,32,560]{3,2,1,0:T(8,128)S(1)} %bitcast.74, f32[1,8,32,560]{3,2,1,0:T(8,128)} %reshape.150), kind=kLoop, calls=%fused_computation.9 | loop fusion | flops 286720 | bytes 1433600 | tf_op jit(solution)/shard_map/convert_element_type | solution.py:50
  (5 shorter events, 0.0 us)
Async XLA Ops:
  6.5 3.1 %copy-start = (bf16[4,10,112,112]{3,2,1,0:T(8,128)(2,1)S(1)}, bf16[4,10,112,112]{3,2,1,0:T(8,128)(2,1)}, u32[]{:S(2)}) copy-start(bf16[4,10,112,112]{3,2,1,0:T(8,128)(2,1)} %param.6) | copy-start | bytes 3010564
  6.5 25.2 %all-reduce.2.cloned.1.call-start = ((), (), s32[]{:S(2)}) async-start(), calls=%async_computation.2 | async-start | bytes 1146880 | tf_op jit(solution)/shard_map/psum | solution.py:59
  34.5 1.9 %copy-start.2 = (bf16[1,4,32,1120]{3,2,1,0:T(8,128)(2,1)S(1)}, bf16[1,4,32,1120]{3,2,1,0:T(8,128)(2,1)}, u32[]{:S(2)}) copy-start(bf16[1,4,32,1120]{3,2,1,0:T(8,128)(2,1)} %param.5) | copy-start | bytes 860164
  54.5 1.4 %copy-start.1 = (f32[4,256,5,112]{1,3,0,2:T(8,128)}, f32[4,256,5,112]{1,3,0,2:T(8,128)S(1)}, u32[]{:S(2)}) copy-start(f32[4,256,5,112]{1,3,0,2:T(8,128)S(1)} %convolution_bitcast_fusion) | copy-start | bytes 6881284
Sparse Core Ops, SparseCore 0:
  11.4 20.3 all-reduce.1
where the time goes:
time: 120 us; the launch traced here: 119 us
  blocking collectives  44.3 us (37%)
  waiting for transfers between devices  20.5 us (17%)
  local copies, waits for them, and re-layouts  20.1 us (17%)
  other arithmetic  13.8 us (12%)
  between operations  13.6 us (11%)
  matrix products  6.67 us (6%)
    all_gather x1, blocking collectives, prefix(): gathered = lax.all_gather(x.astype(jnp.bfloat16), axis)  28.5 us
    psum x1, waiting for transfers between devices, body(): frame_state = lax.psum(local_state(key_rows, value_rows), 'row')  20.5 us
    all_to_all x1, blocking collectives, body(): lax.all_to_all(mixed_video, 'row', split_axis=3, concat_axis=1, tiled=True)  10.2 us
    add x7, other arithmetic, add_states(): return earlier + later  6.6 us
    unnamed x10, local copies, waits for them, and re-layouts  6.55 us
    all_to_all x1, blocking collectives, body(): lax.all_to_all(normed_c, 'row', split_axis=3, concat_axis=1, tiled=True)  5.67 us
    dot_general x2, matrix products, attend(): jnp.einsum('thd,hde->the', queries.astype(jnp.float32), state, precision=...  3.21 us
    mul x2, local copies, waits for them, and re-layouts, finish(): branch = (gating * attended * inv_rms).reshape(frame_block.shape)  3.07 us
  transfers between devices with their start and end apart: 1, of which 1 were waited for; matrix products, arithmetic and copies ran while one was open for 0% of the time, Pallas kernels for 0%

commit v1 on v0

--- a/solution.py
+++ b/solution.py
@@ -61,7 +61,12 @@
     normed_c = normalize(mixed_video)
     mixed_heads, normed_heads = (
         lax.all_to_all(mixed_video, "row", split_axis=3, concat_axis=1, tiled=True),
-        lax.all_to_all(normed_c, "row", split_axis=3, concat_axis=1, tiled=True),
+        jnp.concatenate(
+            lax.all_to_all(
+                jnp.stack(jnp.split(normed_c, lax.axis_size("row"), axis=3)), "row", 0, 0
+            ),
+            axis=1,
+        ),
     )
     head_part = causal_weights.shape[1] // lax.axis_size("row")
     head_start = lax.axis_index("row") * head_part

time: 120 us -> 110 us (0.917)
  local copies, waits for them, and re-layouts: 20.1 us -> 12.3 us
  blocking collectives: 44.3 us -> 42.6 us
    unnamed x10 -> x8, local copies, waits for them, and re-layouts: 6.55 us -> 3.07 us
    convert_element_type x1 -> x0, local copies, waits for them, and re-layouts: 2.2 us -> none  [normalize(): return normed.astype(jnp.bfloat16).reshape(frame_block.shape)]
    all_to_all x1, blocking collectives: 5.67 us -> 3.88 us  [body(): lax.all_to_all(jnp.stack(jnp.split(normed_c, lax.axis_size('row'), axis=3...]
    reshape x1 -> x0, local copies, waits for them, and re-layouts: 1.37 us -> none  [project(): normed = normed.reshape(-1, head_count, head_size)]
    all_to_all x1 -> x0, local copies, waits for them, and re-layouts: 1.36 us -> none  [body(): lax.all_to_all(normed_c, 'row', split_axis=3, concat_axis=1, tiled=True)]
where the time goes in v1:
time: 110 us; the launch traced here: 109 us
  blocking collectives  42.6 us (39%)
  waiting for transfers between devices  20.5 us (19%)
  between operations  13.6 us (12%)
  other arithmetic  13.2 us (12%)
  local copies, waits for them, and re-layouts  12.3 us (11%)
  matrix products  6.67 us (6%)
    all_gather x1, blocking collectives, prefix(): gathered = lax.all_gather(x.astype(jnp.bfloat16), axis)  28.5 us
    psum x1, waiting for transfers between devices, body(): frame_state = lax.psum(local_state(key_rows, value_rows), 'row')  20.5 us
    all_to_all x1, blocking collectives, body(): lax.all_to_all(mixed_video, 'row', split_axis=3, concat_axis=1, tiled=True)  10.2 us
    add x7, other arithmetic, add_states(): return earlier + later  6.6 us
    all_to_all x1, blocking collectives, body(): lax.all_to_all(jnp.stack(jnp.split(normed_c, lax.axis_size('row'), axis=3...  3.88 us
    dot_general x2, matrix products, attend(): jnp.einsum('thd,hde->the', queries.astype(jnp.float32), state, precision=...  3.21 us
    mul x2, local copies, waits for them, and re-layouts, finish(): branch = (gating * attended * inv_rms).reshape(frame_block.shape)  3.07 us
    unnamed x8, local copies, waits for them, and re-layouts  3.07 us
  transfers between devices with their start and end apart: 1, of which 1 were waited for; matrix products, arithmetic and copies ran while one was open for 0% of the time, Pallas kernels for 0%

profile of v1, /device:TPU:27, one launch (start us, length us, event | category | flops | bytes accessed | tf_op | source)
XLA Modules:
  0.0 109.0 jit_solution(2301317136984265872)
XLA Ops:
  6.5 0.0 copy-start
  6.5 0.0 all-reduce.2.cloned.1.call-start
  6.5 1.6 %reshape.147 = f32[128,10,112]{2,1,0:T(8,128)S(1)} reshape(bf16[1,4,32,1120]{3,2,1,0:T(8,128)(2,1)} %param.5) | data formatting | bytes 860160 | tf_op jit(solution)/shard_map/convert_element_type | solution.py:20
  8.2 1.1 %multiply_reduce_fusion = f32[4,32]{1,0:T(4,128)S(1)} fusion(bf16[1,4,32,1120]{3,2,1,0:T(8,128)(2,1)} %param.5), kind=kLoop, calls=%fused_computation.13 | loop fusion | flops 429952 | bytes 287232 | tf_op jit(solution)/shard_map/reduce_sum | solution.py:21
  9.3 0.1 rsqrt.36
  9.4 0.2 fusion.20
  9.6 0.0 copy-done
  9.6 0.5 convolution_bitcast_fusion.1
  10.1 1.1 %fusion.24 = f32[10,112,112]{2,1,0:T(8,128)} fusion(f32[4,128,10,112]{1,3,0,2:T(8,128)S(1)} %convolution_bitcast_fusion.1), kind=kOutput, calls=%fused_computation.46 | convolution fusion | flops 32542720 | bytes 1075200 | tf_op jit(solution)/shard_map/thd,the->hde/dot_general | solution.py:38
  11.3 0.0 all-reduce.2.cloned.1.call-update
  11.3 20.5 %all-reduce.2.cloned.1.call-done = f32[10,112,112]{2,1,0:T(8,128)} async-done(((f32[10,112,112]{2,1,0:T(8,128)}), f32[10,112,112]{2,1,0:T(8,128)}) %all-reduce.2.cloned.1.call-update) | async-done | bytes 501776 | tf_op jit(solution)/shard_map/psum | solution.py:59
  31.8 1.7 %multiply_reduce_fusion.2 = (f32[128,10]{0,1:T(8,128)S(1)}, f32[128,10,112]{0,2,1:T(8,128)S(1)}) fusion(f32[10,112,112]{2,1,0:T(8,128)} %all-reduce.2.cloned.1.call-done, f32[4,128,10,112]{1,3,0,2:T(8,128)S(1)} %convolution_bitcast_fusion.1), kind=kOutput, calls=%fused_computation.40 | convolution fusion | flops 193391360 | bytes 1367040 | tf_op jit(solution)/shard_map/thd,hde->the/dot_general | solution.py:42
  33.5 1.0 fusion.18
  34.5 0.0 copy-start.2
  34.5 1.6 %copy.23 = f32[128,10,112]{2,1,0:T(8,128)S(1)} copy(f32[128,10,112]{0,2,1:T(8,128)} %fusion.18) | data formatting | bytes 1146880 | tf_op jit(solution)/shard_map/mul | solution.py:49
  36.1 0.3 reshape.143
  36.4 0.0 copy-done.2
  36.4 0.2 fusion.1
  36.6 1.4 %copy.24 = bf16[1,4,32,1120]{2,1,0,3:T(4,128)(2,1)S(1)} copy(bf16[1,4,32,1120]{3,2,1,0:T(8,128)(2,1)S(1)} %get-tuple-element.38) | data formatting | bytes 573440 | tf_op jit(solution)/shard_map/convert_element_type | solution.py:50
  38.0 0.1 fusion.2
  38.1 0.1 slice_bitcast_fusion.1
  38.2 0.1 pad_maximum_fusion
  38.3 3.9 %all_to_all.14 = bf16[2,1,4,32,560]{4,3,2,1,0:T(8,128)(2,1)S(1)} all-to-all(bf16[2,1,4,32,560]{4,3,2,1,0:T(8,128)(2,1)S(1)} %pad_maximum_fusion), channel_id=1, replica_groups=mesh['group'=2,'frame'=8,'row'=2] {'row'}, dimensions={0} | all-to-all | bytes 573440 | tf_op jit(solution)/shard_map/all_to_all | solution.py:65
  42.2 0.4 reshape_reshape.4
  42.6 1.6 %convolution_bitcast_fusion = f32[4,256,5,112]{1,3,0,2:T(8,128)S(1)} fusion(bf16[256,5,112,1]{2,1,0,3:T(8,128)(2,1)S(1)} %bitcast.73, bf16[4,10,112,112]{3,2,1,0:T(8,128)(2,1)} %param.7, s32[]{:T(128)S(6)} %select_n.7), kind=kOutput, calls=%fused_computation.1 | convolution fusion | flops 128450560 | bytes 3153924 | tf_op jit(solution)/shard_map/thd,khde->kthe/dot_general | solution.py:29
  44.1 0.0 copy-start.1
  44.2 1.4 %copy-done.1 = f32[4,256,5,112]{1,3,0,2:T(8,128)} copy-done((f32[4,256,5,112]{1,3,0,2:T(8,128)}, f32[4,256,5,112]{1,3,0,2:T(8,128)S(1)}, u32[]{:S(2)}) %copy-start.1) | copy-done | bytes 2293784
  45.5 0.2 fusion.46
  45.8 0.3 convert_element_type.131
  46.0 28.5 %all_gather.4 = bf16[8,490,128]{2,1,0:T(8,128)(2,1)} all-gather(bf16[1,490,128]{2,1,0:T(8,128)(2,1)S(1)} %convert_element_type.131), channel_id=1, replica_groups=mesh['group'=2,'frame'=8,'row'=2] {'frame'}, dimensions={0}, use_global_device_ids=true | all-gather | bytes 1128960 | tf_op jit(solution)/shard_map/all_gather | solution.py:9
  74.6 6.8 %while.10 = (s32[]{:T(128)}, f32[490,128]{1,0:T(8,128)S(1)}, s32[]{:T(128)}, bf16[8,490,128]{2,1,0:T(8,128)(2,1)}, s32[]{:T(128)}, /*index=5*/s32[]{:T(128)}, s32[]{:T(128)}) while((s32[]{:T(128)}, f32[490,128]{1,0:T(8,128)S(1)}, s32[]{:T(128)}, bf16[8,490,128]{2,1,0:T(8,128)(2,1)}, s32[]{:T(128)}, /*index=5*/s32[]{:T(128)}, s32[]{:T(128)}) %tuple.23), condition=%wide.region_5.6_spmd, body=%wide.region_4.5_spmd.sunk | while | flops 125445 | bytes 627315 | solution.py:15
  74.6 0.9 convert_add_fusion.2
  75.6 0.9 convert_add_fusion.2
  76.6 0.9 convert_add_fusion.2
  77.5 0.9 convert_add_fusion.2
  78.5 0.9 convert_add_fusion.2
  79.5 0.9 convert_add_fusion.2
  80.4 0.9 convert_add_fusion.2
  81.4 0.2 reshape.144
  81.6 1.5 %multiply_reduce_fusion.1 = (f32[256,5]{0,1:T(8,128)S(1)}, f32[256,5,112]{0,2,1:T(8,128)S(1)}) fusion(f32[4,256,5,112]{1,3,0,2:T(8,128)} %copy-done.1, f32[5,112,112]{2,1,0:T(8,128)S(1)} %reshape.144, f32[5,112,112]{2,1,0:T(8,128)S(1)} %get-tuple-element.44), kind=kOutput, calls=%fused_computation.39 | convolution fusion | flops 193454080 | bytes 1367040 | tf_op jit(solution)/shard_map/thd,hde->the/dot_general | solution.py:42
  83.1 2.0 %fusion.10 = f32[256,5,112]{0,2,1:T(8,128)} fusion(f32[256,5,112]{0,2,1:T(8,128)S(1)} %get-tuple-element.46, f32[4,256,5,112]{1,3,0,2:T(8,128)} %copy-done.1, f32[256,5]{0,1:T(8,128)S(1)} %add_rsqrt_fusion), kind=kLoop, calls=%fused_computation.25 | loop fusion | flops 716800 | bytes 1725440 | tf_op jit(solution)/shard_map/mul | solution.py:49
  85.1 1.5 %copy.29 = f32[256,5,112]{2,1,0:T(8,128)S(1)} copy(f32[256,5,112]{0,2,1:T(8,128)} %fusion.10) | data formatting | bytes 1146880 | tf_op jit(solution)/shard_map/mul | solution.py:49
  86.6 1.1 reshape.145
  87.7 1.1 %reshape.152 = bf16[2,2,35840]{2,1,0:T(2,128)(2,1)S(1)} reshape(bf16[1120,1,4,32]{3,2,1,0:T(4,128)(2,1)S(1)} %bitcast.71) | data formatting | bytes 573440
  88.8 10.2 %all_to_all.15 = bf16[2,2,35840]{2,1,0:T(2,128)(2,1)S(1)} all-to-all(bf16[2,2,35840]{2,1,0:T(2,128)(2,1)S(1)} %reshape.152), channel_id=1, replica_groups=mesh['group'=2,'frame'=8,'row'=2] {'row'}, dimensions={0} | all-to-all | bytes 573440 | tf_op jit(solution)/shard_map/all_to_all | solution.py:63
  99.0 0.6 reshape.153
  99.5 0.7 copy.25
  100.2 1.9 %add_convert_fusion = bf16[1,8,32,560]{3,2,1,0:T(8,128)(2,1)} fusion(f32[1,8,32,560]{3,2,1,0:T(8,128)S(1)} %bitcast.72, f32[1,8,32,560]{3,2,1,0:T(8,128)} %reshape.145), kind=kLoop, calls=%fused_computation.9 | loop fusion | flops 286720 | bytes 1433600 | tf_op jit(solution)/shard_map/convert_element_type | solution.py:50
  (5 shorter events, 0.0 us)
Async XLA Ops:
  6.5 3.1 %copy-start = (bf16[4,10,112,112]{3,2,1,0:T(8,128)(2,1)S(1)}, bf16[4,10,112,112]{3,2,1,0:T(8,128)(2,1)}, u32[]{:S(2)}) copy-start(bf16[4,10,112,112]{3,2,1,0:T(8,128)(2,1)} %param.6) | copy-start | bytes 3010564
  6.5 25.2 %all-reduce.2.cloned.1.call-start = ((), (), s32[]{:S(2)}) async-start(), calls=%async_computation.2 | async-start | bytes 1146880 | tf_op jit(solution)/shard_map/psum | solution.py:59
  34.5 1.9 %copy-start.2 = (bf16[1,4,32,1120]{3,2,1,0:T(8,128)(2,1)S(1)}, bf16[1,4,32,1120]{3,2,1,0:T(8,128)(2,1)}, u32[]{:S(2)}) copy-start(bf16[1,4,32,1120]{3,2,1,0:T(8,128)(2,1)} %param.5) | copy-start | bytes 860164
  44.1 1.4 %copy-start.1 = (f32[4,256,5,112]{1,3,0,2:T(8,128)}, f32[4,256,5,112]{1,3,0,2:T(8,128)S(1)}, u32[]{:S(2)}) copy-start(f32[4,256,5,112]{1,3,0,2:T(8,128)S(1)} %convolution_bitcast_fusion) | copy-start | bytes 6881284
Sparse Core Ops, SparseCore 0:
  11.4 20.3 all-reduce.1
